TPU v7x, 32 devices: a whole 2x2x4 slice. The times are simulated.
32 devices in a mesh: groups: 2 (over y), space: 4 (over z), inst: 2 (over x), row: 2 (over core).
Axes of the slice: x: 2, y: 2, z: 4, core: 2. Of those that a mesh axis runs over, the one named last changes fastest.
Arguments:
- solution: bfloat16 [2, 4, 320, 8192], P('row', 'inst', None, ('groups', 'space')), parts along dimension 3, may hold values from -6 to 6
- forcing: bfloat16 [2, 4, 320, 8192], P('row', 'inst', None, ('groups', 'space')), parts along dimension 3, may hold values from -6 to 6
- metric_scale: float32 [2, 8192], P('row', ('groups', 'space')), parts along dimension 1, may hold values from 0.5 to 2
- frequency: float32 [1], replicated, may hold values from 0.1 to 0.4
- adjacency: int32 [2, 6, 8192], P('row', None, ('groups', 'space')), parts along dimension 2, may hold values from 0 to 1151, as said below
- partner: int32 [2, 4, 512], P('row', 'inst', ('groups', 'space')), parts along dimension 2, may hold values from 0 to 255, as said below
- volume_matrix: bfloat16 [320, 320], replicated, may hold values from -0.3125 to 0.3125
- trace_matrix: bfloat16 [480, 320], replicated, may hold values from -0.3125 to 0.3125
- lift_matrix: bfloat16 [320, 480], replicated, may hold values from -0.25 to 0.25
- block_inverse: bfloat16 [320, 320], replicated, may hold values from -0.3125 to 0.3125
Outputs:
- updated: bfloat16 [2, 4, 320, 8192], P('row', 'inst', None, ('groups', 'space')), parts along dimension 3
There are 2 independent parts, one for each index of `groups`. A program takes and returns all parts, laid end to end along the dimension named above; an argument that names none is the same for every part. Nothing has to cross between parts.
Inputs may be any that keep to these rules, and one draw needn't show every extreme that they name: The element beside e across face f is (e - e % 1024 - 64 + adjacency[s, f, e]) mod 4096 of the same section, never e itself; the relation is mutual (the element beside e across f has e beside it across face f xor 1); faces 0 to 3 stay within e's block of 1024 elements, and faces 4 and 5 leave it only from the first or the last 64 elements of a block. partner[0, n] is a permutation of the 256 interface rows and partner[1, n] its inverse; for every instance, exactly 16 of the rows k with the same k // 64 map to each block of 64 rows.
All inputs are finite; a program needn't handle non-finite values.
Results may differ from a plain program's by a relative error of at most 0.0054.
Values may be sent and summed in bfloat16 or wider, within the bound.
A program may use at most 64 MiB of HBM per device.

v0:
```python
import functools

import jax
import jax.numpy as jnp
import numpy as np
from jax import lax
from jax.experimental import pallas as pl
from jax.experimental.pallas import tpu as pltpu
from jax.sharding import PartitionSpec as P

LAYER = 64
LANES = 128
CHUNK = 128
TILE = 256
OPPOSITE = (1, 0, 3, 2, 5, 4)
MESH = pl.DeviceIdType.MESH


def spectral_constants(instances):
    positions = np.arange(instances)
    distance = (positions[:, None] - positions[None, :]).astype(np.float32)
    parity = (1.0 - 2.0 * np.mod(positions[:, None] + positions[None, :], 2)).astype(np.float32)
    angles = (np.float32(np.pi) * distance / np.float32(instances)).astype(np.float32)
    sine_values = np.where(distance == 0.0, np.float32(1.0), np.sin(angles))
    cotangent = np.where(distance == 0.0, np.float32(0.0), np.cos(angles) / sine_values)
    return (np.float32(0.5) * parity * cotangent).astype(np.float32)


def one_hot(ids, first, rows):
    numbers = lax.broadcasted_iota(jnp.int32, (rows, ids.shape[1]), 0) + first
    return jnp.where(numbers == ids, 1.0, 0.0).astype(jnp.bfloat16)


def mm(a, b):
    return jnp.dot(a, b, preferred_element_type=jnp.float32)


def kernel(
    insts,
    shards,
    frequency,
    table_hbm,
    scales_hbm,
    adjacency_hbm,
    partner_hbm,
    solution_hbm,
    forcing_hbm,
    volume_hbm,
    trace_hbm,
    lift_hbm,
    inverse_hbm,
    result,
    table,
    scales,
    adjacency,
    partner,
    current,
    forcing,
    volume_matrix,
    trace_turned,
    trace_matrix,
    lift_matrix,
    inverse,
    others,
    traces,
    beside,
    partial,
    low_halo,
    high_halo,
    crossed,
    load_sem,
    inst_send,
    inst_recv,
    halo_send,
    halo_recv,
    cross_send,
    cross_recv,
    above,
    ready,
    met,
):
    local, dof, elements = current.shape
    width = trace_matrix.shape[0] // 6
    iface = partner.shape[2]
    chunks = elements // CHUNK
    my_inst = lax.axis_index("inst")
    my_space = lax.axis_index("space")
    section = lax.axis_index("row")
    right = lax.rem(my_space + 1, shards)
    left = lax.rem(my_space + shards - 1, shards)

    barrier = pltpu.get_barrier_semaphore()
    def signal(semaphore, target):
        pl.semaphore_signal(semaphore, inc=1, device_id=target, device_id_type=MESH)

    other_row = {"row": 1 - section}
    for k in range(1, insts):
        signal(barrier, {"inst": lax.rem(my_inst + k, insts)})
    signal(barrier, other_row)

    @pl.when(my_space < shards - 1)
    def _():
        signal(barrier, {"space": my_space + 1})

    loads = []
    for number, (source, target) in enumerate(
        (
            (trace_hbm, trace_turned),
            (solution_hbm.at[0], current),
            (volume_hbm, volume_matrix),
            (lift_hbm, lift_matrix),
            (forcing_hbm.at[0], forcing),
            (inverse_hbm, inverse),
            (adjacency_hbm, adjacency),
            (partner_hbm, partner),
            (scales_hbm, scales),
            (table_hbm, table),
        )
    ):
        copy = pltpu.make_async_copy(source, target, load_sem.at[number])
        copy.start()
        loads.append(copy)

    pl.semaphore_wait(barrier, insts + jnp.minimum(my_space, 1))

    def inst_copy(k, c):
        columns = pl.ds(pl.multiple_of(c * CHUNK, CHUNK), CHUNK)
        return pltpu.make_async_remote_copy(
            src_ref=solution_hbm.at[0, :, :, columns],
            dst_ref=others.at[k - 1, :, :, columns],
            send_sem=inst_send.at[k - 1, c],
            recv_sem=inst_recv.at[k - 1, c],
            device_id={"inst": lax.rem(my_inst + k, insts)},
            device_id_type=MESH,
        )

    for c in range(chunks):
        for k in range(1, insts):
            inst_copy(k, c).start()

    @pl.when(my_space == shards - 1)
    def _():
        signal(above, {"space": my_space - 1})

    loads[0].wait()
    trace_matrix[...] = trace_turned[...].T
    loads[1].wait()

    def trace_tile(t, carry):
        columns = pl.ds(pl.multiple_of(t * TILE, TILE), TILE)
        for n in range(local):
            values = mm(trace_matrix[...], current[n, :, columns]).astype(jnp.bfloat16)
            for f in range(6):
                traces[f, n * width : (n + 1) * width, columns] = values[
                    f * width : (f + 1) * width
                ]
        return carry

    lax.fori_loop(0, elements // TILE, trace_tile, 0)

    @pl.when(my_space < shards - 1)
    def _():
        pl.semaphore_wait(above, 1)

    @pl.when(jnp.logical_and(my_space > 0, my_space < shards - 1))
    def _():
        signal(above, {"space": my_space - 1})

    @pl.when(my_space == 0)
    def _():
        for j in range(1, shards):
            signal(ready, {"space": j})

    loads[2].wait()

    def volume_tile(t, carry):
        columns = pl.ds(pl.multiple_of(t * TILE, TILE), TILE)
        for n in range(local):
            partial[n, :, columns] = mm(volume_matrix[...], current[n, :, columns])
        return carry

    lax.fori_loop(0, elements // TILE, volume_tile, 0)

    @pl.when(my_space > 0)
    def _():
        pl.semaphore_wait(ready, 1)

    signal(met, other_row)
    pl.semaphore_wait(met, 1)

    to_left = pltpu.make_async_remote_copy(
        src_ref=traces.at[4:6, :, 0:LANES],
        dst_ref=high_halo,
        send_sem=halo_send.at[0],
        recv_sem=halo_recv.at[0],
        device_id={"space": left},
        device_id_type=MESH,
    )
    to_right = pltpu.make_async_remote_copy(
        src_ref=traces.at[4:6, :, elements - LANES : elements],
        dst_ref=low_halo,
        send_sem=halo_send.at[1],
        recv_sem=halo_recv.at[1],
        device_id={"space": right},
        device_id_type=MESH,
    )
    to_left.start()
    to_right.start()

    def cross_copy(j, slot):
        return pltpu.make_async_remote_copy(
            src_ref=traces.at[1 - section, :, 0:LANES],
            dst_ref=crossed.at[slot],
            send_sem=cross_send.at[j],
            recv_sem=cross_recv.at[slot],
            device_id={"space": j, "row": 1 - section},
            device_id_type=MESH,
        )

    for j in range(shards):
        cross_copy(j, my_space).start()

    def put(face, columns, values):
        for n in range(local):
            beside[n, face * width : (face + 1) * width, columns] = values[
                n * width : (n + 1) * width
            ].astype(jnp.bfloat16)

    for copy in loads[6:]:
        copy.wait()
    for face in range(6):

        def gather_tile(t, carry, face=face):
            columns = pl.ds(pl.multiple_of(t * TILE, TILE), TILE)
            ids = adjacency[face, :, columns]
            put(face, columns, mm(traces[OPPOSITE[face]], one_hot(ids, LAYER, elements)))
            return carry

        lax.fori_loop(0, elements // TILE, gather_tile, 0)

    to_left.wait()
    to_right.wait()
    ends = (0,) if elements == LANES else (0, elements - LANES)
    for face in (4, 5):
        for start in ends:
            columns = pl.ds(start, LANES)
            ids = adjacency[face, :, columns]
            facing = OPPOSITE[face] - 4
            low = mm(low_halo[facing], one_hot(ids, LAYER - LANES, LANES))
            high = mm(high_halo[facing], one_hot(ids, LAYER + elements, LANES))
            for n in range(local):
                rows = slice(face * width, (face + 1) * width)
                lines = slice(n * width, (n + 1) * width)
                beside[n, rows, columns] = (
                    beside[n, rows, columns].astype(jnp.float32) + low[lines] + high[lines]
                ).astype(jnp.bfloat16)

    for j in range(shards):
        cross_copy(j, j).wait()
    for n in range(local):
        ids = partner[0, n : n + 1, :]
        lines = slice(n * width, (n + 1) * width)
        total = jnp.zeros((width, iface), jnp.float32)
        for j in range(shards):
            hot = one_hot(ids, j * iface, iface)
            total += mm(crossed[j, lines, 0:iface], hot)
        incoming = total.astype(jnp.bfloat16)
        for face in range(2):
            rows = slice(face * width, (face + 1) * width)
            beside[n, rows, 0:iface] = jnp.where(
                section == 1 - face, incoming, beside[n, rows, 0:iface]
            )

    loads[3].wait()
    loads[4].wait()
    loads[5].wait()

    def lift_tile(t, carry):
        columns = pl.ds(pl.multiple_of(t * TILE, TILE), TILE)
        for n in range(local):
            coupled = mm(lift_matrix[...], beside[n, :, columns])
            partial[n, :, columns] = forcing[n, :, columns].astype(jnp.float32) - scales[
                :, columns
            ] * (partial[n, :, columns] + coupled)
        return carry

    lax.fori_loop(0, elements // TILE, lift_tile, 0)

    factor = frequency[0]
    all_inst = local * insts

    def final_chunk(c, carry):
        columns = pl.ds(pl.multiple_of(c * CHUNK, CHUNK), CHUNK)
        for k in range(1, insts):
            inst_copy(k, c).wait_recv()
        residuals = []
        for n in range(local):
            line = (my_inst * local + n) * all_inst
            source = jnp.zeros((dof, CHUNK), jnp.float32)
            for k in range(insts):
                owner = lax.rem(my_inst + insts - k, insts)
                for m in range(local):
                    values = current[m, :, columns] if k == 0 else others[k - 1, m, :, columns]
                    weight = factor * table[line + owner * local + m]
                    source += weight * values.astype(jnp.float32)
            source = source.astype(jnp.bfloat16).astype(jnp.float32)
            residuals.append((partial[n, :, columns] - source).astype(jnp.bfloat16))
        update = mm(inverse[...], jnp.concatenate(residuals, axis=1))
        inverse_scale = 1.0 / scales[:, columns]
        for n in range(local):
            result[0, n, :, columns] = (
                current[n, :, columns].astype(jnp.float32)
                + update[:, n * CHUNK : (n + 1) * CHUNK] * inverse_scale
            ).astype(jnp.bfloat16)
        return carry

    lax.fori_loop(0, chunks, final_chunk, 0)

    for c in range(chunks):
        for k in range(1, insts):
            inst_copy(k, c).wait_send()


def body(
    solution,
    forcing,
    metric_scale,
    frequency,
    adjacency,
    partner,
    volume_matrix,
    trace_matrix,
    lift_matrix,
    block_inverse,
):
    insts = lax.axis_size("inst")
    shards = lax.axis_size("space")
    _, local, dof, elements = solution.shape
    width = trace_matrix.shape[0] // 6
    chunks = elements // CHUNK
    table = jnp.asarray(spectral_constants(local * insts).reshape(-1))
    vmem = pl.BlockSpec(memory_space=pltpu.VMEM)
    away = pl.BlockSpec(memory_space=pltpu.HBM)
    narrow = jnp.bfloat16
    grant = 67043328 - 2 * solution.size - 65536
    dma = pltpu.SemaphoreType.DMA
    return pl.pallas_call(
        functools.partial(kernel, insts, shards),
        name="sweep",
        out_shape=pltpu.VMEM(solution.shape, narrow),
        in_specs=[pl.BlockSpec(memory_space=pltpu.SMEM)] + [away] * 10,
        out_specs=vmem,
        scratch_shapes=[
            pltpu.SMEM(table.shape, jnp.float32),
            pltpu.VMEM(metric_scale.shape, jnp.float32),
            pltpu.VMEM((6, 1, elements), jnp.int32),
            pltpu.VMEM(partner.shape, jnp.int32),
            pltpu.VMEM((local, dof, elements), narrow),
            pltpu.VMEM((local, dof, elements), narrow),
            pltpu.VMEM(volume_matrix.shape, narrow),
            pltpu.VMEM(trace_matrix.shape[::-1], narrow),
            pltpu.VMEM(trace_matrix.shape, narrow),
            pltpu.VMEM(lift_matrix.shape, narrow),
            pltpu.VMEM(block_inverse.shape, narrow),
            pltpu.VMEM((max(insts - 1, 1), local, dof, elements), narrow),
            pltpu.VMEM((6, local * width, elements), narrow),
            pltpu.VMEM((local, 6 * width, elements), narrow),
            pltpu.VMEM((local, dof, elements), jnp.float32),
            pltpu.VMEM((2, local * width, LANES), narrow),
            pltpu.VMEM((2, local * width, LANES), narrow),
            pltpu.VMEM((shards, local * width, LANES), narrow),
            dma((10,)),
            dma((max(insts - 1, 1), chunks)),
            dma((max(insts - 1, 1), chunks)),
            dma((2,)),
            dma((2,)),
            dma((shards,)),
            dma((shards,)),
            pltpu.SemaphoreType.REGULAR,
            pltpu.SemaphoreType.REGULAR,
            pltpu.SemaphoreType.REGULAR,
        ],
        compiler_params=pltpu.CompilerParams(
            collective_id=0, has_side_effects=True, vmem_limit_bytes=grant
        ),
    )(
        frequency,
        table,
        metric_scale,
        jnp.transpose(adjacency, (1, 0, 2)),
        partner,
        solution,
        forcing,
        volume_matrix,
        trace_matrix.T,
        lift_matrix,
        block_inverse,
    )


def solution(mesh):
    in_specs = (
        P("row", "inst", None, ("groups", "space")),
        P("row", "inst", None, ("groups", "space")),
        P("row", ("groups", "space")),
        P(),
        P("row", None, ("groups", "space")),
        P("row", "inst", ("groups", "space")),
        P(),
        P(),
        P(),
        P(),
    )
    out_specs = P("row", "inst", None, ("groups", "space"))
    return jax.shard_map(body, mesh=mesh, in_specs=in_specs, out_specs=out_specs, check_vma=False)
```

profile of v0, /device:TPU:0, one launch (start us, length us, event | category | flops | bytes accessed | tf_op | source)
XLA Modules:
  0.0 35.1 jit_solution(14577846884726650248)
XLA Ops:
  0.7 33.4 %sweep.1 = bf16[1,2,320,1024]{3,2,1,0:T(8,128)(2,1)S(1)} custom-call(f32[1]{0:T(128)S(6)} %copy.14.frequency, f32[16]{0:T(128)} %constant.2.clone.table_hbm, f32[1,1024]{1,0:T(1,128)} %scales_hbm.1, s32[6,1,1024]{2,1,0:T(1,128)} %bitcast.3, s32[1,2,64]{2,1,0:T(2,128)} %partner_hbm.1, bf16[1,2,320,1024]{3,2,1,0:T(8,128)(2,1)} %solution_hbm.1, ...), custom_call_target="tpu_custom_call" | custom-call | tf_op jit(solution)/shard_map/sweep/pallas_call | solution.py:347
  34.0 1.1 %copy.13 = bf16[1,2,320,1024]{3,2,1,0:T(8,128)(2,1)} copy(bf16[1,2,320,1024]{3,2,1,0:T(8,128)(2,1)S(1)} %sweep.1) | data formatting | bytes 2621440
where the time goes:
time: 35.3 us; the launch traced here: 35.1 us
  Pallas kernels  33.4 us (95%)
  local copies, waits for them, and re-layouts  1.06 us (3%)
  between operations  0.66 us (2%)
    pallas_call x1, Pallas kernels, body(): pl.pallas_call(functools.partial(kernel, insts, shards), name='sweep', ou...  33.4 us
    unnamed x1, local copies, waits for them, and re-layouts  1.06 us

commit v1 on v0

--- a/solution.py
+++ b/solution.py
@@ -65,8 +65,7 @@
     traces,
     beside,
     partial,
-    low_halo,
-    high_halo,
+    halos,
     crossed,
     load_sem,
     inst_send,
@@ -78,11 +77,12 @@
     above,
     ready,
     met,
+    opened,
 ):
     local, dof, elements = current.shape
     width = trace_matrix.shape[0] // 6
     iface = partner.shape[2]
-    chunks = elements // CHUNK
+    parts = split(local, elements)
     my_inst = lax.axis_index("inst")
     my_space = lax.axis_index("space")
     section = lax.axis_index("row")
@@ -93,14 +93,37 @@
     def signal(semaphore, target):
         pl.semaphore_signal(semaphore, inc=1, device_id=target, device_id_type=MESH)
 
+    leads = my_inst == 0
     other_row = {"row": 1 - section}
-    for k in range(1, insts):
-        signal(barrier, {"inst": lax.rem(my_inst + k, insts)})
-    signal(barrier, other_row)
-
-    @pl.when(my_space < shards - 1)
+    peers = [{"inst": lax.rem(my_inst + k, insts)} for k in range(1, insts)]
+    for peer in peers:
+        signal(barrier, peer)
+
+    @pl.when(leads)
+    def _():
+        signal(barrier, other_row)
+
+    @pl.when(jnp.logical_and(leads, my_space < shards - 1))
     def _():
         signal(barrier, {"space": my_space + 1})
+
+    greeted = jnp.where(leads, 1 + jnp.minimum(my_space, 1), 0)
+    pl.semaphore_wait(barrier, insts - 1 + greeted)
+
+    def inst_copy(k, part):
+        picked, start, stop = parts[part]
+        return pltpu.make_async_remote_copy(
+            src_ref=solution_hbm.at[0, picked, :, start:stop],
+            dst_ref=others.at[k - 1, picked, :, start:stop],
+            send_sem=inst_send.at[k - 1],
+            recv_sem=inst_recv.at[k - 1, part],
+            device_id={"inst": lax.rem(my_inst + k, insts)},
+            device_id_type=MESH,
+        )
+
+    for part in range(len(parts)):
+        for k in range(1, insts):
+            inst_copy(k, part).start()
 
     loads = []
     for number, (source, target) in enumerate(
@@ -117,28 +140,11 @@
             (table_hbm, table),
         )
     ):
-        copy = pltpu.make_async_copy(source, target, load_sem.at[number])
+        copy = pltpu.make_async_copy(source, target, load_sem.at[min(number, 3)])
         copy.start()
         loads.append(copy)
 
-    pl.semaphore_wait(barrier, insts + jnp.minimum(my_space, 1))
-
-    def inst_copy(k, c):
-        columns = pl.ds(pl.multiple_of(c * CHUNK, CHUNK), CHUNK)
-        return pltpu.make_async_remote_copy(
-            src_ref=solution_hbm.at[0, :, :, columns],
-            dst_ref=others.at[k - 1, :, :, columns],
-            send_sem=inst_send.at[k - 1, c],
-            recv_sem=inst_recv.at[k - 1, c],
-            device_id={"inst": lax.rem(my_inst + k, insts)},
-            device_id_type=MESH,
-        )
-
-    for c in range(chunks):
-        for k in range(1, insts):
-            inst_copy(k, c).start()
-
-    @pl.when(my_space == shards - 1)
+    @pl.when(jnp.logical_and(leads, my_space == shards - 1))
     def _():
         signal(above, {"space": my_space - 1})
 
@@ -158,15 +164,15 @@
 
     lax.fori_loop(0, elements // TILE, trace_tile, 0)
 
-    @pl.when(my_space < shards - 1)
+    @pl.when(jnp.logical_and(leads, my_space < shards - 1))
     def _():
         pl.semaphore_wait(above, 1)
 
-    @pl.when(jnp.logical_and(my_space > 0, my_space < shards - 1))
+    @pl.when(jnp.logical_and(leads, jnp.logical_and(my_space > 0, my_space < shards - 1)))
     def _():
         signal(above, {"space": my_space - 1})
 
-    @pl.when(my_space == 0)
+    @pl.when(jnp.logical_and(leads, my_space == 0))
     def _():
         for j in range(1, shards):
             signal(ready, {"space": j})
@@ -181,26 +187,34 @@
 
     lax.fori_loop(0, elements // TILE, volume_tile, 0)
 
-    @pl.when(my_space > 0)
+    @pl.when(jnp.logical_and(leads, my_space > 0))
     def _():
         pl.semaphore_wait(ready, 1)
 
-    signal(met, other_row)
-    pl.semaphore_wait(met, 1)
+    @pl.when(leads)
+    def _():
+        signal(met, other_row)
+        pl.semaphore_wait(met, 1)
+        for peer in peers:
+            signal(opened, peer)
+
+    @pl.when(jnp.logical_not(leads))
+    def _():
+        pl.semaphore_wait(opened, 1)
 
     to_left = pltpu.make_async_remote_copy(
         src_ref=traces.at[4:6, :, 0:LANES],
-        dst_ref=high_halo,
-        send_sem=halo_send.at[0],
-        recv_sem=halo_recv.at[0],
+        dst_ref=halos.at[1],
+        send_sem=halo_send,
+        recv_sem=halo_recv,
         device_id={"space": left},
         device_id_type=MESH,
     )
     to_right = pltpu.make_async_remote_copy(
         src_ref=traces.at[4:6, :, elements - LANES : elements],
-        dst_ref=low_halo,
-        send_sem=halo_send.at[1],
-        recv_sem=halo_recv.at[1],
+        dst_ref=halos.at[0],
+        send_sem=halo_send,
+        recv_sem=halo_recv,
         device_id={"space": right},
         device_id_type=MESH,
     )
@@ -211,8 +225,8 @@
         return pltpu.make_async_remote_copy(
             src_ref=traces.at[1 - section, :, 0:LANES],
             dst_ref=crossed.at[slot],
-            send_sem=cross_send.at[j],
-            recv_sem=cross_recv.at[slot],
+            send_sem=cross_send,
+            recv_sem=cross_recv,
             device_id={"space": j, "row": 1 - section},
             device_id_type=MESH,
         )
@@ -226,7 +240,7 @@
                 n * width : (n + 1) * width
             ].astype(jnp.bfloat16)
 
-    for copy in loads[6:]:
+    for copy in loads[3:]:
         copy.wait()
     for face in range(6):
 
@@ -238,16 +252,23 @@
 
         lax.fori_loop(0, elements // TILE, gather_tile, 0)
 
-    to_left.wait()
-    to_right.wait()
+    both = pltpu.make_async_remote_copy(
+        src_ref=halos,
+        dst_ref=halos,
+        send_sem=halo_send,
+        recv_sem=halo_recv,
+        device_id={"space": left},
+        device_id_type=MESH,
+    )
+    both.wait()
     ends = (0,) if elements == LANES else (0, elements - LANES)
     for face in (4, 5):
         for start in ends:
             columns = pl.ds(start, LANES)
             ids = adjacency[face, :, columns]
             facing = OPPOSITE[face] - 4
-            low = mm(low_halo[facing], one_hot(ids, LAYER - LANES, LANES))
-            high = mm(high_halo[facing], one_hot(ids, LAYER + elements, LANES))
+            low = mm(halos[0, facing], one_hot(ids, LAYER - LANES, LANES))
+            high = mm(halos[1, facing], one_hot(ids, LAYER + elements, LANES))
             for n in range(local):
                 rows = slice(face * width, (face + 1) * width)
                 lines = slice(n * width, (n + 1) * width)
@@ -255,8 +276,15 @@
                     beside[n, rows, columns].astype(jnp.float32) + low[lines] + high[lines]
                 ).astype(jnp.bfloat16)
 
-    for j in range(shards):
-        cross_copy(j, j).wait()
+    every = pltpu.make_async_remote_copy(
+        src_ref=crossed,
+        dst_ref=crossed,
+        send_sem=cross_send,
+        recv_sem=cross_recv,
+        device_id={"row": 1 - section},
+        device_id_type=MESH,
+    )
+    every.wait()
     for n in range(local):
         ids = partner[0, n : n + 1, :]
         lines = slice(n * width, (n + 1) * width)
@@ -271,54 +299,77 @@
                 section == 1 - face, incoming, beside[n, rows, 0:iface]
             )
 
-    loads[3].wait()
-    loads[4].wait()
-    loads[5].wait()
+    factor = frequency[0]
+    all_inst = local * insts
+
+    def weight(n, owner, m):
+        return factor * table[(my_inst * local + n) * all_inst + owner * local + m]
 
     def lift_tile(t, carry):
         columns = pl.ds(pl.multiple_of(t * TILE, TILE), TILE)
+        scale = scales[:, columns]
+        inverse_scale = 1.0 / scale
         for n in range(local):
             coupled = mm(lift_matrix[...], beside[n, :, columns])
-            partial[n, :, columns] = forcing[n, :, columns].astype(jnp.float32) - scales[
-                :, columns
-            ] * (partial[n, :, columns] + coupled)
+            residual = forcing[n, :, columns].astype(jnp.float32) - scale * (
+                partial[n, :, columns] + coupled
+            )
+            for m in range(local):
+                residual -= weight(n, my_inst, m) * current[m, :, columns].astype(jnp.float32)
+            update = mm(inverse[...], residual.astype(jnp.bfloat16))
+            partial[n, :, columns] = (
+                current[n, :, columns].astype(jnp.float32) + update * inverse_scale
+            )
         return carry
 
     lax.fori_loop(0, elements // TILE, lift_tile, 0)
 
-    factor = frequency[0]
-    all_inst = local * insts
-
-    def final_chunk(c, carry):
-        columns = pl.ds(pl.multiple_of(c * CHUNK, CHUNK), CHUNK)
+    for part, (picked, start, stop) in enumerate(parts):
+        chosen = range(local)[picked]
+        wide = min(TILE, stop - start)
         for k in range(1, insts):
-            inst_copy(k, c).wait_recv()
-        residuals = []
-        for n in range(local):
-            line = (my_inst * local + n) * all_inst
-            source = jnp.zeros((dof, CHUNK), jnp.float32)
-            for k in range(insts):
-                owner = lax.rem(my_inst + insts - k, insts)
-                for m in range(local):
-                    values = current[m, :, columns] if k == 0 else others[k - 1, m, :, columns]
-                    weight = factor * table[line + owner * local + m]
-                    source += weight * values.astype(jnp.float32)
-            source = source.astype(jnp.bfloat16).astype(jnp.float32)
-            residuals.append((partial[n, :, columns] - source).astype(jnp.bfloat16))
-        update = mm(inverse[...], jnp.concatenate(residuals, axis=1))
-        inverse_scale = 1.0 / scales[:, columns]
-        for n in range(local):
-            result[0, n, :, columns] = (
-                current[n, :, columns].astype(jnp.float32)
-                + update[:, n * CHUNK : (n + 1) * CHUNK] * inverse_scale
-            ).astype(jnp.bfloat16)
-        return carry
-
-    lax.fori_loop(0, chunks, final_chunk, 0)
-
-    for c in range(chunks):
-        for k in range(1, insts):
-            inst_copy(k, c).wait_send()
+            owner = lax.rem(my_inst + insts - k, insts)
+            last = k == insts - 1 and chosen[-1] == local - 1
+            inst_copy(k, part).wait_recv()
+
+            def turn_tile(t, carry):
+                columns = pl.ds(pl.multiple_of(start + t * wide, wide), wide)
+                inverse_scale = 1.0 / scales[:, columns]
+                values = [partial[n, :, columns] for n in range(local)]
+                for m in chosen:
+                    update = mm(inverse[...], others[k - 1, m, :, columns]) * inverse_scale
+                    values = [values[n] - weight(n, owner, m) * update for n in range(local)]
+                for n in range(local):
+                    if last:
+                        result[0, n, :, columns] = values[n].astype(jnp.bfloat16)
+                    else:
+                        partial[n, :, columns] = values[n]
+                return carry
+
+            lax.fori_loop(0, (stop - start) // wide, turn_tile, 0)
+
+    if insts == 1:
+        result[0] = partial[...].astype(jnp.bfloat16)
+
+    for k in range(1, insts):
+        pltpu.make_async_remote_copy(
+            src_ref=solution_hbm.at[0],
+            dst_ref=others.at[k - 1],
+            send_sem=inst_send.at[k - 1],
+            recv_sem=inst_recv.at[k - 1, 0],
+            device_id={"inst": lax.rem(my_inst + k, insts)},
+            device_id_type=MESH,
+        ).wait_send()
+
+
+def split(local, elements):
+    parts = []
+    start = 0
+    while elements - start > CHUNK:
+        stop = start + max(CHUNK, (elements - start) // (2 * CHUNK) * CHUNK)
+        parts.append((slice(0, local), start, stop))
+        start = stop
+    return parts + [(slice(m, m + 1), start, elements) for m in range(local)]
 
 
 def body(
@@ -337,7 +388,7 @@
     shards = lax.axis_size("space")
     _, local, dof, elements = solution.shape
     width = trace_matrix.shape[0] // 6
-    chunks = elements // CHUNK
+    parts = split(local, elements)
     table = jnp.asarray(spectral_constants(local * insts).reshape(-1))
     vmem = pl.BlockSpec(memory_space=pltpu.VMEM)
     away = pl.BlockSpec(memory_space=pltpu.HBM)
@@ -366,16 +417,16 @@
             pltpu.VMEM((6, local * width, elements), narrow),
             pltpu.VMEM((local, 6 * width, elements), narrow),
             pltpu.VMEM((local, dof, elements), jnp.float32),
-            pltpu.VMEM((2, local * width, LANES), narrow),
-            pltpu.VMEM((2, local * width, LANES), narrow),
+            pltpu.VMEM((2, 2, local * width, LANES), narrow),
             pltpu.VMEM((shards, local * width, LANES), narrow),
-            dma((10,)),
-            dma((max(insts - 1, 1), chunks)),
-            dma((max(insts - 1, 1), chunks)),
-            dma((2,)),
-            dma((2,)),
-            dma((shards,)),
-            dma((shards,)),
+            dma((4,)),
+            dma((max(insts - 1, 1),)),
+            dma((max(insts - 1, 1), len(parts))),
+            dma,
+            dma,
+            dma,
+            dma,
+            pltpu.SemaphoreType.REGULAR,
             pltpu.SemaphoreType.REGULAR,
             pltpu.SemaphoreType.REGULAR,
             pltpu.SemaphoreType.REGULAR,

time: 35.3 us -> 34.3 us (0.972)
  Pallas kernels: 33.4 us -> 32.4 us
    pallas_call x1, Pallas kernels: 33.4 us -> 32.4 us  [body(): pl.pallas_call(functools.partial(kernel, insts, shards), name='sweep', ou...]
where the time goes in v1:
time: 34.3 us; the launch traced here: 34.1 us
  Pallas kernels  32.4 us (94%)
  local copies, waits for them, and re-layouts  1.06 us (3%)
  between operations  0.66 us (2%)
    pallas_call x1, Pallas kernels, body(): pl.pallas_call(functools.partial(kernel, insts, shards), name='sweep', ou...  32.4 us
    unnamed x1, local copies, waits for them, and re-layouts  1.06 us

profile of v1, /device:TPU:0, one launch (start us, length us, event | category | flops | bytes accessed | tf_op | source)
XLA Modules:
  0.0 34.1 jit_solution(14897983682322621030)
XLA Ops:
  0.7 32.4 %sweep.1 = bf16[1,2,320,1024]{3,2,1,0:T(8,128)(2,1)S(1)} custom-call(f32[1]{0:T(128)S(6)} %copy.14.frequency, f32[16]{0:T(128)} %constant.2.clone.table_hbm, f32[1,1024]{1,0:T(1,128)} %scales_hbm.1, s32[6,1,1024]{2,1,0:T(1,128)} %bitcast.3, s32[1,2,64]{2,1,0:T(2,128)} %partner_hbm.1, bf16[1,2,320,1024]{3,2,1,0:T(8,128)(2,1)} %solution_hbm.1, ...), custom_call_target="tpu_custom_call" | custom-call | tf_op jit(solution)/shard_map/sweep/pallas_call | solution.py:398
  33.1 1.1 %copy.13 = bf16[1,2,320,1024]{3,2,1,0:T(8,128)(2,1)} copy(bf16[1,2,320,1024]{3,2,1,0:T(8,128)(2,1)S(1)} %sweep.1) | data formatting | bytes 2621440

commit v2 on v1

--- a/solution.py
+++ b/solution.py
@@ -78,6 +78,10 @@
     ready,
     met,
     opened,
+    relayed,
+    relay_send,
+    relay_recv,
+    onward_send,
 ):
     local, dof, elements = current.shape
     width = trace_matrix.shape[0] // 6
@@ -121,9 +125,41 @@
             device_id_type=MESH,
         )
 
-    for part in range(len(parts)):
-        for k in range(1, insts):
-            inst_copy(k, part).start()
+    early = range(1, 2 + min(local - 1, 1))
+    late = range(early.stop, len(parts))
+
+    def send(numbers):
+        for part in numbers:
+            for k in range(1, insts):
+                inst_copy(k, part).start()
+
+    @pl.when(section == 0)
+    def _():
+        send(early)
+        send(late)
+
+    @pl.when(section == 1)
+    def _():
+        send(range(early.stop))
+
+    relay = pltpu.make_async_remote_copy(
+        src_ref=solution_hbm.at[0, 0, :, 0:CHUNK],
+        dst_ref=relayed,
+        send_sem=relay_send,
+        recv_sem=relay_recv,
+        device_id=other_row,
+        device_id_type=MESH,
+    )
+
+    def onward(k):
+        return pltpu.make_async_remote_copy(
+            src_ref=relayed,
+            dst_ref=others.at[k - 1, 0, :, 0:CHUNK],
+            send_sem=onward_send,
+            recv_sem=inst_recv.at[k - 1, 0],
+            device_id={"inst": lax.rem(my_inst + k, insts), "row": 0},
+            device_id_type=MESH,
+        )
 
     loads = []
     for number, (source, target) in enumerate(
@@ -202,6 +238,10 @@
     def _():
         pl.semaphore_wait(opened, 1)
 
+    @pl.when(section == 0)
+    def _():
+        relay.start()
+
     to_left = pltpu.make_async_remote_copy(
         src_ref=traces.at[4:6, :, 0:LANES],
         dst_ref=halos.at[1],
@@ -251,6 +291,14 @@
             return carry
 
         lax.fori_loop(0, elements // TILE, gather_tile, 0)
+        if face == 1:
+
+            @pl.when(section == 1)
+            def _():
+                relay.wait_recv()
+                for k in range(1, insts):
+                    onward(k).start()
+                send(late)
 
     both = pltpu.make_async_remote_copy(
         src_ref=halos,
@@ -326,7 +374,7 @@
 
     for part, (picked, start, stop) in enumerate(parts):
         chosen = range(local)[picked]
-        wide = min(TILE, stop - start)
+        wide = TILE if (stop - start) % TILE == 0 else CHUNK
         for k in range(1, insts):
             owner = lax.rem(my_inst + insts - k, insts)
             last = k == insts - 1 and chosen[-1] == local - 1
@@ -351,20 +399,37 @@
     if insts == 1:
         result[0] = partial[...].astype(jnp.bfloat16)
 
-    for k in range(1, insts):
+    def sent(source, semaphore):
         pltpu.make_async_remote_copy(
-            src_ref=solution_hbm.at[0],
-            dst_ref=others.at[k - 1],
-            send_sem=inst_send.at[k - 1],
-            recv_sem=inst_recv.at[k - 1, 0],
-            device_id={"inst": lax.rem(my_inst + k, insts)},
+            src_ref=source,
+            dst_ref=source,
+            send_sem=semaphore,
+            recv_sem=relay_recv,
+            device_id=other_row,
             device_id_type=MESH,
         ).wait_send()
 
+    @pl.when(section == 0)
+    def _():
+        sent(relayed, relay_send)
+        for k in range(1, insts):
+            sent(others.at[k - 1, 0, :, CHUNK:], inst_send.at[k - 1])
+            if local > 1:
+                sent(others.at[k - 1, 1:], inst_send.at[k - 1])
+
+    @pl.when(section == 1)
+    def _():
+        sent(others.at[:, 0, :, 0:CHUNK], onward_send)
+        for k in range(1, insts):
+            sent(others.at[k - 1], inst_send.at[k - 1])
+
 
 def split(local, elements):
-    parts = []
-    start = 0
+    half = elements // (2 * CHUNK) * CHUNK
+    parts = [(slice(0, 1), 0, CHUNK), (slice(0, 1), CHUNK, half)]
+    if local > 1:
+        parts.append((slice(1, local), 0, half))
+    start = half
     while elements - start > CHUNK:
         stop = start + max(CHUNK, (elements - start) // (2 * CHUNK) * CHUNK)
         parts.append((slice(0, local), start, stop))
@@ -430,6 +495,10 @@
             pltpu.SemaphoreType.REGULAR,
             pltpu.SemaphoreType.REGULAR,
             pltpu.SemaphoreType.REGULAR,
+            pltpu.VMEM((dof, CHUNK), narrow),
+            dma,
+            dma,
+            dma,
         ],
         compiler_params=pltpu.CompilerParams(
             collective_id=0, has_side_effects=True, vmem_limit_bytes=grant

time: 34.3 us -> 33.7 us (0.983)
  Pallas kernels: 32.4 us -> 31.5 us
    pallas_call x1, Pallas kernels: 32.4 us -> 31.5 us  [body(): pl.pallas_call(functools.partial(kernel, insts, shards), name='sweep', ou...]
where the time goes in v2:
time: 33.7 us; the launch traced here: 33.2 us
  Pallas kernels  31.5 us (93%)
  local copies, waits for them, and re-layouts  1.06 us (3%)
  between operations  0.66 us (2%)
    pallas_call x1, Pallas kernels, body(): pl.pallas_call(functools.partial(kernel, insts, shards), name='sweep', ou...  31.5 us
    unnamed x1, local copies, waits for them, and re-layouts  1.06 us

profile of v2, /device:TPU:0, one launch (start us, length us, event | category | flops | bytes accessed | tf_op | source)
XLA Modules:
  0.0 33.2 jit_solution(18229018839845985335)
XLA Ops:
  0.7 31.5 %sweep.1 = bf16[1,2,320,1024]{3,2,1,0:T(8,128)(2,1)S(1)} custom-call(f32[1]{0:T(128)S(6)} %copy.14.frequency, f32[16]{0:T(128)} %constant.2.clone.table_hbm, f32[1,1024]{1,0:T(1,128)} %scales_hbm.1, s32[6,1,1024]{2,1,0:T(1,128)} %bitcast.3, s32[1,2,64]{2,1,0:T(2,128)} %partner_hbm.1, bf16[1,2,320,1024]{3,2,1,0:T(8,128)(2,1)} %solution_hbm.1, ...), custom_call_target="tpu_custom_call" | custom-call | tf_op jit(solution)/shard_map/sweep/pallas_call | solution.py:463
  32.2 1.1 %copy.13 = bf16[1,2,320,1024]{3,2,1,0:T(8,128)(2,1)} copy(bf16[1,2,320,1024]{3,2,1,0:T(8,128)(2,1)S(1)} %sweep.1) | data formatting | bytes 2621440

commit v3 on v2

--- a/solution.py
+++ b/solution.py
@@ -38,7 +38,7 @@
 def kernel(
     insts,
     shards,
-    frequency,
+    given,
     table_hbm,
     scales_hbm,
     adjacency_hbm,
@@ -68,20 +68,18 @@
     halos,
     crossed,
     load_sem,
-    inst_send,
+    sending,
     inst_recv,
-    halo_send,
     halo_recv,
-    cross_send,
     cross_recv,
     above,
     ready,
     met,
     opened,
     relayed,
-    relay_send,
     relay_recv,
-    onward_send,
+    frequency,
+    frequency_recv,
 ):
     local, dof, elements = current.shape
     width = trace_matrix.shape[0] // 6
@@ -119,7 +117,7 @@
         return pltpu.make_async_remote_copy(
             src_ref=solution_hbm.at[0, picked, :, start:stop],
             dst_ref=others.at[k - 1, picked, :, start:stop],
-            send_sem=inst_send.at[k - 1],
+            send_sem=sending,
             recv_sem=inst_recv.at[k - 1, part],
             device_id={"inst": lax.rem(my_inst + k, insts)},
             device_id_type=MESH,
@@ -133,6 +131,21 @@
             for k in range(1, insts):
                 inst_copy(k, part).start()
 
+    def share(k):
+        return pltpu.make_async_remote_copy(
+            src_ref=given,
+            dst_ref=frequency,
+            send_sem=sending,
+            recv_sem=frequency_recv,
+            device_id=peers[k - 1],
+            device_id_type=MESH,
+        )
+
+    @pl.when(leads)
+    def _():
+        for k in range(1, insts):
+            share(k).start()
+
     @pl.when(section == 0)
     def _():
         send(early)
@@ -145,7 +158,7 @@
     relay = pltpu.make_async_remote_copy(
         src_ref=solution_hbm.at[0, 0, :, 0:CHUNK],
         dst_ref=relayed,
-        send_sem=relay_send,
+        send_sem=sending,
         recv_sem=relay_recv,
         device_id=other_row,
         device_id_type=MESH,
@@ -155,7 +168,7 @@
         return pltpu.make_async_remote_copy(
             src_ref=relayed,
             dst_ref=others.at[k - 1, 0, :, 0:CHUNK],
-            send_sem=onward_send,
+            send_sem=sending,
             recv_sem=inst_recv.at[k - 1, 0],
             device_id={"inst": lax.rem(my_inst + k, insts), "row": 0},
             device_id_type=MESH,
@@ -176,7 +189,7 @@
             (table_hbm, table),
         )
     ):
-        copy = pltpu.make_async_copy(source, target, load_sem.at[min(number, 3)])
+        copy = pltpu.make_async_copy(source, target, load_sem.at[min(number // 3, 1)])
         copy.start()
         loads.append(copy)
 
@@ -184,9 +197,9 @@
     def _():
         signal(above, {"space": my_space - 1})
 
-    loads[0].wait()
+    for copy in loads[:3]:
+        copy.wait()
     trace_matrix[...] = trace_turned[...].T
-    loads[1].wait()
 
     def trace_tile(t, carry):
         columns = pl.ds(pl.multiple_of(t * TILE, TILE), TILE)
@@ -213,8 +226,6 @@
         for j in range(1, shards):
             signal(ready, {"space": j})
 
-    loads[2].wait()
-
     def volume_tile(t, carry):
         columns = pl.ds(pl.multiple_of(t * TILE, TILE), TILE)
         for n in range(local):
@@ -245,7 +256,7 @@
     to_left = pltpu.make_async_remote_copy(
         src_ref=traces.at[4:6, :, 0:LANES],
         dst_ref=halos.at[1],
-        send_sem=halo_send,
+        send_sem=sending,
         recv_sem=halo_recv,
         device_id={"space": left},
         device_id_type=MESH,
@@ -253,7 +264,7 @@
     to_right = pltpu.make_async_remote_copy(
         src_ref=traces.at[4:6, :, elements - LANES : elements],
         dst_ref=halos.at[0],
-        send_sem=halo_send,
+        send_sem=sending,
         recv_sem=halo_recv,
         device_id={"space": right},
         device_id_type=MESH,
@@ -265,7 +276,7 @@
         return pltpu.make_async_remote_copy(
             src_ref=traces.at[1 - section, :, 0:LANES],
             dst_ref=crossed.at[slot],
-            send_sem=cross_send,
+            send_sem=sending,
             recv_sem=cross_recv,
             device_id={"space": j, "row": 1 - section},
             device_id_type=MESH,
@@ -303,12 +314,12 @@
     both = pltpu.make_async_remote_copy(
         src_ref=halos,
         dst_ref=halos,
-        send_sem=halo_send,
+        send_sem=sending,
         recv_sem=halo_recv,
         device_id={"space": left},
         device_id_type=MESH,
     )
-    both.wait()
+    both.wait_recv()
     ends = (0,) if elements == LANES else (0, elements - LANES)
     for face in (4, 5):
         for start in ends:
@@ -327,12 +338,12 @@
     every = pltpu.make_async_remote_copy(
         src_ref=crossed,
         dst_ref=crossed,
-        send_sem=cross_send,
+        send_sem=sending,
         recv_sem=cross_recv,
         device_id={"row": 1 - section},
         device_id_type=MESH,
     )
-    every.wait()
+    every.wait_recv()
     for n in range(local):
         ids = partner[0, n : n + 1, :]
         lines = slice(n * width, (n + 1) * width)
@@ -347,7 +358,18 @@
                 section == 1 - face, incoming, beside[n, rows, 0:iface]
             )
 
-    factor = frequency[0]
+
+    @pl.when(leads)
+    def _():
+        frequency[...] = given[...]
+
+    if insts > 1:
+
+        @pl.when(jnp.logical_not(leads))
+        def _():
+            share(1).wait_recv()
+
+    factor = frequency[0:1, 0:1]
     all_inst = local * insts
 
     def weight(n, owner, m):
@@ -399,29 +421,35 @@
     if insts == 1:
         result[0] = partial[...].astype(jnp.bfloat16)
 
-    def sent(source, semaphore):
+    both.wait_send()
+    every.wait_send()
+
+    def sent(source):
         pltpu.make_async_remote_copy(
             src_ref=source,
             dst_ref=source,
-            send_sem=semaphore,
+            send_sem=sending,
             recv_sem=relay_recv,
             device_id=other_row,
             device_id_type=MESH,
         ).wait_send()
 
+    @pl.when(leads)
+    def _():
+        for _ in peers:
+            sent(frequency)
+
     @pl.when(section == 0)
     def _():
-        sent(relayed, relay_send)
-        for k in range(1, insts):
-            sent(others.at[k - 1, 0, :, CHUNK:], inst_send.at[k - 1])
-            if local > 1:
-                sent(others.at[k - 1, 1:], inst_send.at[k - 1])
+        sent(relayed)
+        sent(others.at[:, 0, :, CHUNK:])
+        if local > 1:
+            sent(others.at[:, 1:])
 
     @pl.when(section == 1)
     def _():
-        sent(others.at[:, 0, :, 0:CHUNK], onward_send)
-        for k in range(1, insts):
-            sent(others.at[k - 1], inst_send.at[k - 1])
+        sent(others.at[:, 0, :, 0:CHUNK])
+        sent(others)
 
 
 def split(local, elements):
@@ -464,7 +492,7 @@
         functools.partial(kernel, insts, shards),
         name="sweep",
         out_shape=pltpu.VMEM(solution.shape, narrow),
-        in_specs=[pl.BlockSpec(memory_space=pltpu.SMEM)] + [away] * 10,
+        in_specs=[vmem] + [away] * 10,
         out_specs=vmem,
         scratch_shapes=[
             pltpu.SMEM(table.shape, jnp.float32),
@@ -484,11 +512,9 @@
             pltpu.VMEM((local, dof, elements), jnp.float32),
             pltpu.VMEM((2, 2, local * width, LANES), narrow),
             pltpu.VMEM((shards, local * width, LANES), narrow),
-            dma((4,)),
-            dma((max(insts - 1, 1),)),
+            dma((2,)),
+            dma,
             dma((max(insts - 1, 1), len(parts))),
-            dma,
-            dma,
             dma,
             dma,
             pltpu.SemaphoreType.REGULAR,
@@ -497,14 +523,19 @@
             pltpu.SemaphoreType.REGULAR,
             pltpu.VMEM((dof, CHUNK), narrow),
             dma,
-            dma,
+            pltpu.VMEM((8, LANES), jnp.float32),
             dma,
         ],
         compiler_params=pltpu.CompilerParams(
             collective_id=0, has_side_effects=True, vmem_limit_bytes=grant
         ),
     )(
-        frequency,
+        lax.cond(
+            lax.axis_index("inst") == 0,
+            lambda value: jnp.broadcast_to(value, (8, LANES)),
+            lambda value: jnp.zeros((8, LANES), jnp.float32),
+            frequency,
+        ),
         table,
         metric_scale,
         jnp.transpose(adjacency, (1, 0, 2)),

time: 33.7 us -> 33 us (0.979)
  Pallas kernels: 31.5 us -> 30.7 us
  between operations: 0.66 us -> 0.02 us
  local copies, waits for them, and re-layouts: 1.06 us -> 1.7 us
    pallas_call x1, Pallas kernels: 31.5 us -> 30.7 us  [body(): pl.pallas_call(functools.partial(kernel, insts, shards), name='sweep', ou...]
    broadcast_in_dim x0 -> x1, local copies, waits for them, and re-layouts: none -> 0.65 us  [body(): jnp.broadcast_to(value, (8, LANES))]
where the time goes in v3:
time: 33 us; the launch traced here: 32.5 us
  Pallas kernels  30.7 us (93%)
  local copies, waits for them, and re-layouts  1.7 us (5%)
    pallas_call x1, Pallas kernels, body(): pl.pallas_call(functools.partial(kernel, insts, shards), name='sweep', ou...  30.7 us
    unnamed x1, local copies, waits for them, and re-layouts  1.06 us

profile of v3, /device:TPU:0, one launch (start us, length us, event | category | flops | bytes accessed | tf_op | source)
XLA Modules:
  0.0 32.5 jit_solution(17194597564385720145)
XLA Ops:
  0.0 0.6 %conditional.1 = (f32[8,128]{1,0:T(8,128)S(1)}) conditional(s32[]{:T(128)} %convert_element_type.3, () %tuple.11, (f32[1]{0:T(128)}) %tuple.12), branch_computations={%region_0.0_spmd, %region_1.0_spmd} | conditional | bytes 4108 | solution.py:533
  0.0 0.6 %broadcast_in_dim.0 = f32[8,128]{1,0:T(8,128)S(1)} broadcast(f32[]{:T(128)} %bitcast), dimensions={} | broadcast | bytes 4100 | tf_op jit(solution)/shard_map/cond/branch_1_fun/broadcast_in_dim | solution.py:535
  0.7 30.7 %sweep.1 = bf16[1,2,320,1024]{3,2,1,0:T(8,128)(2,1)S(1)} custom-call(f32[8,128]{1,0:T(8,128)S(1)} %get-tuple-element.11.given, f32[16]{0:T(128)} %constant.10.clone.table_hbm, f32[1,1024]{1,0:T(1,128)} %scales_hbm.1, s32[6,1,1024]{2,1,0:T(1,128)} %bitcast.4, s32[1,2,64]{2,1,0:T(2,128)} %partner_hbm.1, bf16[1,2,320,1024]{3,2,1,0:T(8,128)(2,1)} %solution_hbm.1, ...), custom_call_target="tpu_custom_call" | custom-call | tf_op jit(solution)/shard_map/sweep/pallas_call | solution.py:491
  31.4 1.1 %copy.16 = bf16[1,2,320,1024]{3,2,1,0:T(8,128)(2,1)} copy(bf16[1,2,320,1024]{3,2,1,0:T(8,128)(2,1)S(1)} %sweep.1) | data formatting | bytes 2621440

commit v4 on v3

--- a/solution.py
+++ b/solution.py
@@ -131,6 +131,8 @@
             for k in range(1, insts):
                 inst_copy(k, part).start()
 
+    holds = jnp.logical_and(leads, section == 0)
+
     def share(k):
         return pltpu.make_async_remote_copy(
             src_ref=given,
@@ -141,7 +143,7 @@
             device_id_type=MESH,
         )
 
-    @pl.when(leads)
+    @pl.when(holds)
     def _():
         for k in range(1, insts):
             share(k).start()
@@ -249,8 +251,28 @@
     def _():
         pl.semaphore_wait(opened, 1)
 
+    across = pltpu.make_async_remote_copy(
+        src_ref=frequency,
+        dst_ref=frequency,
+        send_sem=sending,
+        recv_sem=frequency_recv,
+        device_id=other_row,
+        device_id_type=MESH,
+    )
+
+    @pl.when(holds)
+    def _():
+        frequency[...] = given[...]
+
+    if insts > 1:
+
+        @pl.when(jnp.logical_and(jnp.logical_not(leads), section == 0))
+        def _():
+            share(1).wait_recv()
+
     @pl.when(section == 0)
     def _():
+        across.start()
         relay.start()
 
     to_left = pltpu.make_async_remote_copy(
@@ -359,15 +381,9 @@
             )
 
 
-    @pl.when(leads)
-    def _():
-        frequency[...] = given[...]
-
-    if insts > 1:
-
-        @pl.when(jnp.logical_not(leads))
-        def _():
-            share(1).wait_recv()
+    @pl.when(section == 1)
+    def _():
+        across.wait_recv()
 
     factor = frequency[0:1, 0:1]
     all_inst = local * insts
@@ -434,13 +450,14 @@
             device_id_type=MESH,
         ).wait_send()
 
-    @pl.when(leads)
+    @pl.when(holds)
     def _():
         for _ in peers:
             sent(frequency)
 
     @pl.when(section == 0)
     def _():
+        sent(frequency)
         sent(relayed)
         sent(others.at[:, 0, :, CHUNK:])
         if local > 1:
@@ -531,7 +548,7 @@
         ),
     )(
         lax.cond(
-            lax.axis_index("inst") == 0,
+            jnp.logical_and(lax.axis_index("inst") == 0, lax.axis_index("row") == 0),
             lambda value: jnp.broadcast_to(value, (8, LANES)),
             lambda value: jnp.zeros((8, LANES), jnp.float32),
             frequency,

time: 33 us -> 32.9 us (level)
  no operation moved by 1% of the time
where the time goes in v4:
time: 32.9 us; the launch traced here: 32.5 us
  Pallas kernels  30.8 us (94%)
  local copies, waits for them, and re-layouts  1.7 us (5%)
    pallas_call x1, Pallas kernels, body(): pl.pallas_call(functools.partial(kernel, insts, shards), name='sweep', ou...  30.8 us
    unnamed x1, local copies, waits for them, and re-layouts  1.06 us

profile of v4, /device:TPU:0, one launch (start us, length us, event | category | flops | bytes accessed | tf_op | source)
XLA Modules:
  0.0 32.5 jit_solution(13238267972906253532)
XLA Ops:
  0.0 0.6 %conditional.1 = (f32[8,128]{1,0:T(8,128)S(1)}) conditional(s32[]{:T(128)} %convert_element_type.3, () %tuple.11, (f32[1]{0:T(128)}) %tuple.12), branch_computations={%region_0.0_spmd, %region_1.0_spmd} | conditional | bytes 4108 | solution.py:550
  0.0 0.6 %broadcast_in_dim.0 = f32[8,128]{1,0:T(8,128)S(1)} broadcast(f32[]{:T(128)} %bitcast), dimensions={} | broadcast | bytes 4100 | tf_op jit(solution)/shard_map/cond/branch_1_fun/broadcast_in_dim | solution.py:552
  0.7 30.8 %sweep.1 = bf16[1,2,320,1024]{3,2,1,0:T(8,128)(2,1)S(1)} custom-call(f32[8,128]{1,0:T(8,128)S(1)} %get-tuple-element.11.given, f32[16]{0:T(128)} %constant.12.clone.table_hbm, f32[1,1024]{1,0:T(1,128)} %scales_hbm.1, s32[6,1,1024]{2,1,0:T(1,128)} %bitcast.4, s32[1,2,64]{2,1,0:T(2,128)} %partner_hbm.1, bf16[1,2,320,1024]{3,2,1,0:T(8,128)(2,1)} %solution_hbm.1, ...), custom_call_target="tpu_custom_call" | custom-call | tf_op jit(solution)/shard_map/sweep/pallas_call | solution.py:508
  31.4 1.1 %copy.16 = bf16[1,2,320,1024]{3,2,1,0:T(8,128)(2,1)} copy(bf16[1,2,320,1024]{3,2,1,0:T(8,128)(2,1)S(1)} %sweep.1) | data formatting | bytes 2621440

commit v5 on v4

--- a/solution.py
+++ b/solution.py
@@ -65,21 +65,17 @@
     traces,
     beside,
     partial,
-    halos,
-    crossed,
+    arrived,
     load_sem,
     sending,
     inst_recv,
-    halo_recv,
-    cross_recv,
-    above,
-    ready,
-    met,
-    opened,
+    spread,
+    column,
+    plane,
     relayed,
+    frequency,
+    handed,
     relay_recv,
-    frequency,
-    frequency_recv,
 ):
     local, dof, elements = current.shape
     width = trace_matrix.shape[0] // 6
@@ -112,19 +108,20 @@
     greeted = jnp.where(leads, 1 + jnp.minimum(my_space, 1), 0)
     pl.semaphore_wait(barrier, insts - 1 + greeted)
 
+    early = range(1, 2 + min(local - 1, 1))
+    late = range(early.stop, len(parts))
+
     def inst_copy(k, part):
         picked, start, stop = parts[part]
         return pltpu.make_async_remote_copy(
             src_ref=solution_hbm.at[0, picked, :, start:stop],
             dst_ref=others.at[k - 1, picked, :, start:stop],
             send_sem=sending,
-            recv_sem=inst_recv.at[k - 1, part],
+            recv_sem=inst_recv.at[k - 1, max(part - early.stop + 1, 0)],
             device_id={"inst": lax.rem(my_inst + k, insts)},
             device_id_type=MESH,
         )
 
-    early = range(1, 2 + min(local - 1, 1))
-    late = range(early.stop, len(parts))
 
     def send(numbers):
         for part in numbers:
@@ -138,7 +135,7 @@
             src_ref=given,
             dst_ref=frequency,
             send_sem=sending,
-            recv_sem=frequency_recv,
+            recv_sem=handed,
             device_id=peers[k - 1],
             device_id_type=MESH,
         )
@@ -197,7 +194,7 @@
 
     @pl.when(jnp.logical_and(leads, my_space == shards - 1))
     def _():
-        signal(above, {"space": my_space - 1})
+        signal(column, {"space": my_space - 1})
 
     for copy in loads[:3]:
         copy.wait()
@@ -217,16 +214,16 @@
 
     @pl.when(jnp.logical_and(leads, my_space < shards - 1))
     def _():
-        pl.semaphore_wait(above, 1)
+        pl.semaphore_wait(column, 1)
 
     @pl.when(jnp.logical_and(leads, jnp.logical_and(my_space > 0, my_space < shards - 1)))
     def _():
-        signal(above, {"space": my_space - 1})
+        signal(column, {"space": my_space - 1})
 
     @pl.when(jnp.logical_and(leads, my_space == 0))
     def _():
         for j in range(1, shards):
-            signal(ready, {"space": j})
+            signal(column, {"space": j})
 
     def volume_tile(t, carry):
         columns = pl.ds(pl.multiple_of(t * TILE, TILE), TILE)
@@ -238,24 +235,24 @@
 
     @pl.when(jnp.logical_and(leads, my_space > 0))
     def _():
-        pl.semaphore_wait(ready, 1)
+        pl.semaphore_wait(column, 1)
 
     @pl.when(leads)
     def _():
-        signal(met, other_row)
-        pl.semaphore_wait(met, 1)
+        signal(plane, other_row)
+        pl.semaphore_wait(plane, 1)
         for peer in peers:
-            signal(opened, peer)
+            signal(plane, peer)
 
     @pl.when(jnp.logical_not(leads))
     def _():
-        pl.semaphore_wait(opened, 1)
+        pl.semaphore_wait(plane, 1)
 
     across = pltpu.make_async_remote_copy(
         src_ref=frequency,
         dst_ref=frequency,
         send_sem=sending,
-        recv_sem=frequency_recv,
+        recv_sem=handed,
         device_id=other_row,
         device_id_type=MESH,
     )
@@ -277,17 +274,17 @@
 
     to_left = pltpu.make_async_remote_copy(
         src_ref=traces.at[4:6, :, 0:LANES],
-        dst_ref=halos.at[1],
+        dst_ref=arrived.at[2:4],
         send_sem=sending,
-        recv_sem=halo_recv,
+        recv_sem=spread,
         device_id={"space": left},
         device_id_type=MESH,
     )
     to_right = pltpu.make_async_remote_copy(
         src_ref=traces.at[4:6, :, elements - LANES : elements],
-        dst_ref=halos.at[0],
+        dst_ref=arrived.at[0:2],
         send_sem=sending,
-        recv_sem=halo_recv,
+        recv_sem=spread,
         device_id={"space": right},
         device_id_type=MESH,
     )
@@ -297,9 +294,9 @@
     def cross_copy(j, slot):
         return pltpu.make_async_remote_copy(
             src_ref=traces.at[1 - section, :, 0:LANES],
-            dst_ref=crossed.at[slot],
+            dst_ref=arrived.at[4 + slot],
             send_sem=sending,
-            recv_sem=cross_recv,
+            recv_sem=spread,
             device_id={"space": j, "row": 1 - section},
             device_id_type=MESH,
         )
@@ -329,27 +326,28 @@
             @pl.when(section == 1)
             def _():
                 relay.wait_recv()
+                across.wait_recv()
                 for k in range(1, insts):
                     onward(k).start()
                 send(late)
 
-    both = pltpu.make_async_remote_copy(
-        src_ref=halos,
-        dst_ref=halos,
+    every = pltpu.make_async_remote_copy(
+        src_ref=arrived,
+        dst_ref=arrived,
         send_sem=sending,
-        recv_sem=halo_recv,
-        device_id={"space": left},
+        recv_sem=spread,
+        device_id=other_row,
         device_id_type=MESH,
     )
-    both.wait_recv()
+    every.wait_recv()
     ends = (0,) if elements == LANES else (0, elements - LANES)
     for face in (4, 5):
         for start in ends:
             columns = pl.ds(start, LANES)
             ids = adjacency[face, :, columns]
             facing = OPPOSITE[face] - 4
-            low = mm(halos[0, facing], one_hot(ids, LAYER - LANES, LANES))
-            high = mm(halos[1, facing], one_hot(ids, LAYER + elements, LANES))
+            low = mm(arrived[facing], one_hot(ids, LAYER - LANES, LANES))
+            high = mm(arrived[2 + facing], one_hot(ids, LAYER + elements, LANES))
             for n in range(local):
                 rows = slice(face * width, (face + 1) * width)
                 lines = slice(n * width, (n + 1) * width)
@@ -357,22 +355,13 @@
                     beside[n, rows, columns].astype(jnp.float32) + low[lines] + high[lines]
                 ).astype(jnp.bfloat16)
 
-    every = pltpu.make_async_remote_copy(
-        src_ref=crossed,
-        dst_ref=crossed,
-        send_sem=sending,
-        recv_sem=cross_recv,
-        device_id={"row": 1 - section},
-        device_id_type=MESH,
-    )
-    every.wait_recv()
     for n in range(local):
         ids = partner[0, n : n + 1, :]
         lines = slice(n * width, (n + 1) * width)
         total = jnp.zeros((width, iface), jnp.float32)
         for j in range(shards):
             hot = one_hot(ids, j * iface, iface)
-            total += mm(crossed[j, lines, 0:iface], hot)
+            total += mm(arrived[4 + j, lines, 0:iface], hot)
         incoming = total.astype(jnp.bfloat16)
         for face in range(2):
             rows = slice(face * width, (face + 1) * width)
@@ -380,10 +369,6 @@
                 section == 1 - face, incoming, beside[n, rows, 0:iface]
             )
 
-
-    @pl.when(section == 1)
-    def _():
-        across.wait_recv()
 
     factor = frequency[0:1, 0:1]
     all_inst = local * insts
@@ -410,13 +395,27 @@
 
     lax.fori_loop(0, elements // TILE, lift_tile, 0)
 
+    def first_half(k):
+        block = others.at[k - 1, :, :, 0 : parts[early.stop][1]]
+        return pltpu.make_async_remote_copy(
+            src_ref=block,
+            dst_ref=block,
+            send_sem=sending,
+            recv_sem=inst_recv.at[k - 1, 0],
+            device_id=peers[k - 1],
+            device_id_type=MESH,
+        )
+
     for part, (picked, start, stop) in enumerate(parts):
         chosen = range(local)[picked]
         wide = TILE if (stop - start) % TILE == 0 else CHUNK
         for k in range(1, insts):
             owner = lax.rem(my_inst + insts - k, insts)
             last = k == insts - 1 and chosen[-1] == local - 1
-            inst_copy(k, part).wait_recv()
+            if part == 0:
+                first_half(k).wait_recv()
+            elif part >= early.stop:
+                inst_copy(k, part).wait_recv()
 
             def turn_tile(t, carry):
                 columns = pl.ds(pl.multiple_of(start + t * wide, wide), wide)
@@ -437,7 +436,6 @@
     if insts == 1:
         result[0] = partial[...].astype(jnp.bfloat16)
 
-    both.wait_send()
     every.wait_send()
 
     def sent(source):
@@ -445,7 +443,7 @@
             src_ref=source,
             dst_ref=source,
             send_sem=sending,
-            recv_sem=relay_recv,
+            recv_sem=handed,
             device_id=other_row,
             device_id_type=MESH,
         ).wait_send()
@@ -527,20 +525,16 @@
             pltpu.VMEM((6, local * width, elements), narrow),
             pltpu.VMEM((local, 6 * width, elements), narrow),
             pltpu.VMEM((local, dof, elements), jnp.float32),
-            pltpu.VMEM((2, 2, local * width, LANES), narrow),
-            pltpu.VMEM((shards, local * width, LANES), narrow),
+            pltpu.VMEM((4 + shards, local * width, LANES), narrow),
             dma((2,)),
             dma,
-            dma((max(insts - 1, 1), len(parts))),
-            dma,
+            dma((max(insts - 1, 1), len(parts) - min(local - 1, 1) - 1)),
             dma,
             pltpu.SemaphoreType.REGULAR,
             pltpu.SemaphoreType.REGULAR,
-            pltpu.SemaphoreType.REGULAR,
-            pltpu.SemaphoreType.REGULAR,
             pltpu.VMEM((dof, CHUNK), narrow),
+            pltpu.VMEM((8, LANES), jnp.float32),
             dma,
-            pltpu.VMEM((8, LANES), jnp.float32),
             dma,
         ],
         compiler_params=pltpu.CompilerParams(

time: 32.9 us -> 32.9 us (level)
  no operation moved by 1% of the time
where the time goes in v5:
time: 32.9 us; the launch traced here: 32.4 us
  Pallas kernels  30.7 us (93%)
  local copies, waits for them, and re-layouts  1.7 us (5%)
    pallas_call x1, Pallas kernels, body(): pl.pallas_call(functools.partial(kernel, insts, shards), name='sweep', ou...  30.7 us
    unnamed x1, local copies, waits for them, and re-layouts  1.06 us

profile of v5, /device:TPU:0, one launch (start us, length us, event | category | flops | bytes accessed | tf_op | source)
XLA Modules:
  0.0 32.4 jit_solution(8993005279357971454)
XLA Ops:
  0.0 0.6 %conditional.1 = (f32[8,128]{1,0:T(8,128)S(1)}) conditional(s32[]{:T(128)} %convert_element_type.3, () %tuple.11, (f32[1]{0:T(128)}) %tuple.12), branch_computations={%region_0.0_spmd, %region_1.0_spmd} | conditional | bytes 4108 | solution.py:544
  0.0 0.6 %broadcast_in_dim.0 = f32[8,128]{1,0:T(8,128)S(1)} broadcast(f32[]{:T(128)} %bitcast), dimensions={} | broadcast | bytes 4100 | tf_op jit(solution)/shard_map/cond/branch_1_fun/broadcast_in_dim | solution.py:546
  0.7 30.7 %sweep.1 = bf16[1,2,320,1024]{3,2,1,0:T(8,128)(2,1)S(1)} custom-call(f32[8,128]{1,0:T(8,128)S(1)} %get-tuple-element.11.given, f32[16]{0:T(128)} %constant.12.clone.table_hbm, f32[1,1024]{1,0:T(1,128)} %scales_hbm.1, s32[6,1,1024]{2,1,0:T(1,128)} %bitcast.4, s32[1,2,64]{2,1,0:T(2,128)} %partner_hbm.1, bf16[1,2,320,1024]{3,2,1,0:T(8,128)(2,1)} %solution_hbm.1, ...), custom_call_target="tpu_custom_call" | custom-call | tf_op jit(solution)/shard_map/sweep/pallas_call | solution.py:506
  31.4 1.1 %copy.16 = bf16[1,2,320,1024]{3,2,1,0:T(8,128)(2,1)} copy(bf16[1,2,320,1024]{3,2,1,0:T(8,128)(2,1)S(1)} %sweep.1) | data formatting | bytes 2621440

commit v6 on v5

--- a/solution.py
+++ b/solution.py
@@ -154,22 +154,27 @@
     def _():
         send(range(early.stop))
 
-    relay = pltpu.make_async_remote_copy(
-        src_ref=solution_hbm.at[0, 0, :, 0:CHUNK],
-        dst_ref=relayed,
-        send_sem=sending,
-        recv_sem=relay_recv,
-        device_id=other_row,
-        device_id_type=MESH,
-    )
-
-    def onward(k):
+    final = len(parts) - 1
+
+    def relay(part):
+        picked, start, stop = parts[part]
+        return pltpu.make_async_remote_copy(
+            src_ref=solution_hbm.at[0, picked.start, :, start:stop],
+            dst_ref=relayed,
+            send_sem=sending,
+            recv_sem=relay_recv,
+            device_id=other_row,
+            device_id_type=MESH,
+        )
+
+    def onward(k, part, row):
+        picked, start, stop = parts[part]
         return pltpu.make_async_remote_copy(
             src_ref=relayed,
-            dst_ref=others.at[k - 1, 0, :, 0:CHUNK],
-            send_sem=sending,
-            recv_sem=inst_recv.at[k - 1, 0],
-            device_id={"inst": lax.rem(my_inst + k, insts), "row": 0},
+            dst_ref=others.at[k - 1, picked.start, :, start:stop],
+            send_sem=sending,
+            recv_sem=inst_recv.at[k - 1, max(part - early.stop + 1, 0)],
+            device_id={"inst": lax.rem(my_inst + k, insts), "row": row},
             device_id_type=MESH,
         )
 
@@ -270,7 +275,11 @@
     @pl.when(section == 0)
     def _():
         across.start()
-        relay.start()
+        relay(0).start()
+
+    @pl.when(section == 1)
+    def _():
+        relay(final).start()
 
     to_left = pltpu.make_async_remote_copy(
         src_ref=traces.at[4:6, :, 0:LANES],
@@ -323,13 +332,19 @@
         lax.fori_loop(0, elements // TILE, gather_tile, 0)
         if face == 1:
 
+            relay(0).wait_recv()
+
+            @pl.when(section == 0)
+            def _():
+                for k in range(1, insts):
+                    onward(k, final, 1).start()
+
             @pl.when(section == 1)
             def _():
-                relay.wait_recv()
                 across.wait_recv()
                 for k in range(1, insts):
-                    onward(k).start()
-                send(late)
+                    onward(k, 0, 0).start()
+                send(late[:-1])
 
     every = pltpu.make_async_remote_copy(
         src_ref=arrived,
@@ -456,15 +471,9 @@
     @pl.when(section == 0)
     def _():
         sent(frequency)
-        sent(relayed)
-        sent(others.at[:, 0, :, CHUNK:])
-        if local > 1:
-            sent(others.at[:, 1:])
-
-    @pl.when(section == 1)
-    def _():
-        sent(others.at[:, 0, :, 0:CHUNK])
-        sent(others)
+
+    sent(relayed)
+    sent(others)
 
 
 def split(local, elements):

time: 32.9 us -> 32.9 us (level)
  no operation moved by 1% of the time
where the time goes in v6:
time: 32.9 us; the launch traced here: 32.4 us
  Pallas kernels  30.7 us (93%)
  local copies, waits for them, and re-layouts  1.7 us (5%)
    pallas_call x1, Pallas kernels, body(): pl.pallas_call(functools.partial(kernel, insts, shards), name='sweep', ou...  30.7 us
    unnamed x1, local copies, waits for them, and re-layouts  1.06 us

profile of v6, /device:TPU:0, one launch (start us, length us, event | category | flops | bytes accessed | tf_op | source)
XLA Modules:
  0.0 32.4 jit_solution(705677175134413878)
XLA Ops:
  0.0 0.6 %conditional.1 = (f32[8,128]{1,0:T(8,128)S(1)}) conditional(s32[]{:T(128)} %convert_element_type.3, () %tuple.11, (f32[1]{0:T(128)}) %tuple.12), branch_computations={%region_0.0_spmd, %region_1.0_spmd} | conditional | bytes 4108 | solution.py:553
  0.0 0.6 %broadcast_in_dim.0 = f32[8,128]{1,0:T(8,128)S(1)} broadcast(f32[]{:T(128)} %bitcast), dimensions={} | broadcast | bytes 4100 | tf_op jit(solution)/shard_map/cond/branch_1_fun/broadcast_in_dim | solution.py:555
  0.7 30.7 %sweep.1 = bf16[1,2,320,1024]{3,2,1,0:T(8,128)(2,1)S(1)} custom-call(f32[8,128]{1,0:T(8,128)S(1)} %get-tuple-element.11.given, f32[16]{0:T(128)} %constant.12.clone.table_hbm, f32[1,1024]{1,0:T(1,128)} %scales_hbm.1, s32[6,1,1024]{2,1,0:T(1,128)} %bitcast.4, s32[1,2,64]{2,1,0:T(2,128)} %partner_hbm.1, bf16[1,2,320,1024]{3,2,1,0:T(8,128)(2,1)} %solution_hbm.1, ...), custom_call_target="tpu_custom_call" | custom-call | tf_op jit(solution)/shard_map/sweep/pallas_call | solution.py:515
  31.4 1.1 %copy.16 = bf16[1,2,320,1024]{3,2,1,0:T(8,128)(2,1)} copy(bf16[1,2,320,1024]{3,2,1,0:T(8,128)(2,1)S(1)} %sweep.1) | data formatting | bytes 2621440

commit v7 on v6

--- a/solution.py
+++ b/solution.py
@@ -482,10 +482,9 @@
     if local > 1:
         parts.append((slice(1, local), 0, half))
     start = half
-    while elements - start > CHUNK:
-        stop = start + max(CHUNK, (elements - start) // (2 * CHUNK) * CHUNK)
-        parts.append((slice(0, local), start, stop))
-        start = stop
+    if elements - start > CHUNK:
+        parts.append((slice(0, local), start, elements - CHUNK))
+        start = elements - CHUNK
     return parts + [(slice(m, m + 1), start, elements) for m in range(local)]
 
 

time: 32.9 us -> 32.9 us (level)
  no operation moved by 1% of the time
where the time goes in v7:
time: 32.9 us; the launch traced here: 32.4 us
  Pallas kernels  30.7 us (93%)
  local copies, waits for them, and re-layouts  1.7 us (5%)
    pallas_call x1, Pallas kernels, body(): pl.pallas_call(functools.partial(kernel, insts, shards), name='sweep', ou...  30.7 us
    unnamed x1, local copies, waits for them, and re-layouts  1.06 us

profile of v7, /device:TPU:0, one launch (start us, length us, event | category | flops | bytes accessed | tf_op | source)
XLA Modules:
  0.0 32.4 jit_solution(4807423358667461584)
XLA Ops:
  0.0 0.6 %conditional.1 = (f32[8,128]{1,0:T(8,128)S(1)}) conditional(s32[]{:T(128)} %convert_element_type.3, () %tuple.11, (f32[1]{0:T(128)}) %tuple.12), branch_computations={%region_0.0_spmd, %region_1.0_spmd} | conditional | bytes 4108 | solution.py:552
  0.0 0.6 %broadcast_in_dim.0 = f32[8,128]{1,0:T(8,128)S(1)} broadcast(f32[]{:T(128)} %bitcast), dimensions={} | broadcast | bytes 4100 | tf_op jit(solution)/shard_map/cond/branch_1_fun/broadcast_in_dim | solution.py:554
  0.7 30.7 %sweep.1 = bf16[1,2,320,1024]{3,2,1,0:T(8,128)(2,1)S(1)} custom-call(f32[8,128]{1,0:T(8,128)S(1)} %get-tuple-element.11.given, f32[16]{0:T(128)} %constant.12.clone.table_hbm, f32[1,1024]{1,0:T(1,128)} %scales_hbm.1, s32[6,1,1024]{2,1,0:T(1,128)} %bitcast.4, s32[1,2,64]{2,1,0:T(2,128)} %partner_hbm.1, bf16[1,2,320,1024]{3,2,1,0:T(8,128)(2,1)} %solution_hbm.1, ...), custom_call_target="tpu_custom_call" | custom-call | tf_op jit(solution)/shard_map/sweep/pallas_call | solution.py:514
  31.4 1.1 %copy.16 = bf16[1,2,320,1024]{3,2,1,0:T(8,128)(2,1)} copy(bf16[1,2,320,1024]{3,2,1,0:T(8,128)(2,1)S(1)} %sweep.1) | data formatting | bytes 2621440

commit v8 on v7

--- a/solution.py
+++ b/solution.py
@@ -152,7 +152,16 @@
 
     @pl.when(section == 1)
     def _():
-        send(range(early.stop))
+        columns = slice(0, parts[early.stop][1])
+        for k in range(1, insts):
+            pltpu.make_async_remote_copy(
+                src_ref=solution_hbm.at[0, :, :, columns],
+                dst_ref=others.at[k - 1, :, :, columns],
+                send_sem=sending,
+                recv_sem=inst_recv.at[k - 1, 0],
+                device_id=peers[k - 1],
+                device_id_type=MESH,
+            ).start()
 
     final = len(parts) - 1
 

time: 32.9 us -> 32.9 us (level)
  no operation moved by 1% of the time
where the time goes in v8:
time: 32.9 us; the launch traced here: 32.4 us
  Pallas kernels  30.7 us (93%)
  local copies, waits for them, and re-layouts  1.7 us (5%)
    pallas_call x1, Pallas kernels, body(): pl.pallas_call(functools.partial(kernel, insts, shards), name='sweep', ou...  30.7 us
    unnamed x1, local copies, waits for them, and re-layouts  1.06 us

profile of v8, /device:TPU:0, one launch (start us, length us, event | category | flops | bytes accessed | tf_op | source)
XLA Modules:
  0.0 32.4 jit_solution(10040914362420243942)
XLA Ops:
  0.0 0.6 %conditional.1 = (f32[8,128]{1,0:T(8,128)S(1)}) conditional(s32[]{:T(128)} %convert_element_type.3, () %tuple.11, (f32[1]{0:T(128)}) %tuple.12), branch_computations={%region_0.0_spmd, %region_1.0_spmd} | conditional | bytes 4108 | solution.py:561
  0.0 0.6 %broadcast_in_dim.0 = f32[8,128]{1,0:T(8,128)S(1)} broadcast(f32[]{:T(128)} %bitcast), dimensions={} | broadcast | bytes 4100 | tf_op jit(solution)/shard_map/cond/branch_1_fun/broadcast_in_dim | solution.py:563
  0.7 30.7 %sweep.1 = bf16[1,2,320,1024]{3,2,1,0:T(8,128)(2,1)S(1)} custom-call(f32[8,128]{1,0:T(8,128)S(1)} %get-tuple-element.11.given, f32[16]{0:T(128)} %constant.12.clone.table_hbm, f32[1,1024]{1,0:T(1,128)} %scales_hbm.1, s32[6,1,1024]{2,1,0:T(1,128)} %bitcast.4, s32[1,2,64]{2,1,0:T(2,128)} %partner_hbm.1, bf16[1,2,320,1024]{3,2,1,0:T(8,128)(2,1)} %solution_hbm.1, ...), custom_call_target="tpu_custom_call" | custom-call | tf_op jit(solution)/shard_map/sweep/pallas_call | solution.py:523
  31.4 1.1 %copy.16 = bf16[1,2,320,1024]{3,2,1,0:T(8,128)(2,1)} copy(bf16[1,2,320,1024]{3,2,1,0:T(8,128)(2,1)S(1)} %sweep.1) | data formatting | bytes 2621440
